TPU v7x, 256 devices: a whole 4x4x8 slice. The times are simulated.
256 devices in a mesh: context: 16 (over z, core), heads: 16 (over x, y).
Axes of the slice: x: 4, y: 4, z: 8, core: 2. Of those that a mesh axis runs over, the one named last changes fastest.
Arguments:
- main_query: bfloat16 [256, 128, 576], P('context', 'heads'), may hold values from -6 to 6
- latent_keys: bfloat16 [32768, 576], P('context'), may hold values from -6 to 6
- head_lse: float32 [256, 128], P(None, 'heads'), may hold values from 4 to 8
- lengths: int32 [256], replicated, may hold values from 1 to 32768, as said below
- index_query: bfloat16 [256, 64, 128], P('heads'), may hold values from -256 to 256
- index_key: bfloat16 [32768, 128], P('context'), may hold values from -8 to 8
- index_weight: float32 [256, 64], P('heads'), may hold values from -2.4 to 2.4
Outputs:
- grad_index_query: float32 [256, 64, 128], P('heads', 'context')
- grad_index_key: float32 [32768, 128], P(('context', 'heads'))
Inputs may be any that keep to these rules, and one draw needn't show every extreme that they name: Query rows come in blocks of 16 consecutive rows whose lengths rise by one from row to row; some block ends at the last key.
All inputs are finite; a program needn't handle non-finite values.
Results may differ from a plain program's by a relative error of at most 0.0029.
Values may be sent and summed in bfloat16 or wider, within the bound.
A program may use at most 64 MiB of HBM per device.

v0:
```python
import math
import jax
import jax.numpy as jnp
from jax import lax
from jax.sharding import PartitionSpec as P

main_scale = 192.0 ** (-0.5)
loss_scale = 64.0
masked_low = -1e30


def head_mass(queries, lse_rows, len_rows, latent, first_key):
    row_count = queries.shape[0]
    block_rows = math.gcd(row_count, 64)
    steps_count = row_count // block_rows
    key_pos = first_key + jnp.arange(latent.shape[0], dtype=jnp.int32)

    def one_block(inputs):
        query_block, lse_block, len_block = inputs
        scores = (
            jnp.einsum("rhd,sd->rhs", query_block, latent, preferred_element_type=jnp.float32)
            * main_scale
        )
        summed = jnp.sum(jnp.exp(scores - lse_block[:, :, None]), axis=1)
        return jnp.where(key_pos[None, :] < len_block[:, None], summed, 0.0)

    stacked = lax.map(
        one_block,
        (
            queries.reshape((steps_count, block_rows) + queries.shape[1:]),
            lse_rows.reshape(steps_count, block_rows, lse_rows.shape[1]),
            len_rows.reshape(steps_count, block_rows),
        ),
    )
    return stacked.reshape(row_count, latent.shape[0])


def on_device(main_query, latent_keys, head_lse, lengths, index_query, index_key, index_weight):
    key_count = latent_keys.shape[0]
    first_key = lax.axis_index("context") * key_count
    own_rows = index_query.shape[0]
    row_first = lax.axis_index("heads") * own_rows
    partial_mass = head_mass(
        lax.all_gather(main_query, "context", axis=0, tiled=True),
        head_lse,
        lengths,
        latent_keys,
        first_key,
    )
    summed_mass = lax.psum(partial_mass, "heads")
    row_mass = lax.dynamic_slice_in_dim(summed_mass, row_first, own_rows, 0)
    own_len = lax.dynamic_slice_in_dim(lengths, row_first, own_rows, 0)
    visible = (first_key + jnp.arange(key_count, dtype=jnp.int32))[None, :] < own_len[:, None]
    heads_count = index_query.shape[1]
    width = index_query.shape[2]
    index_scale = width ** (-0.5)
    flat_query = index_query.reshape(own_rows * heads_count, width)
    block_keys = math.gcd(key_count, 512)
    block_total = key_count // block_keys
    key_blocks = index_key.reshape(block_total, block_keys, width)

    def block_dots(key_block):
        products = lax.dot_general(
            flat_query, key_block, (((1,), (1,)), ((), ())), preferred_element_type=jnp.float32
        )
        return products.reshape(own_rows, heads_count, key_block.shape[0])

    def block_logits(key_block):
        return (
            jnp.einsum(
                "tj,tjs->ts",
                index_weight,
                jax.nn.relu(block_dots(key_block)),
                precision=lax.Precision.HIGHEST,
            )
            * index_scale
        )

    logits = jnp.moveaxis(lax.map(block_logits, key_blocks), 0, 1).reshape(own_rows, key_count)
    local_top = jnp.max(jnp.where(visible, logits, masked_low), axis=1)
    mass_local = jnp.sum(row_mass, axis=1)
    top = lax.pmax(local_top, "context")
    weights_exp = jnp.where(visible, jnp.exp(logits - top[:, None]), 0.0)
    share_sum, mass_total = lax.psum((jnp.sum(weights_exp, axis=1), mass_local), "context")
    probability = weights_exp / share_sum[:, None]
    target = row_mass / mass_total[:, None]
    slopes = loss_scale * (probability - target)
    slope_blocks = slopes.reshape(own_rows, block_total, block_keys).transpose(1, 0, 2)

    def back_step(query_grad, inputs):
        key_block, slope_block = inputs
        products = block_dots(key_block)
        terms = jnp.where(
            products > 0, slope_block[:, None, :] * index_weight[:, :, None] * index_scale, 0.0
        )
        terms = terms.astype(jnp.bfloat16).reshape(own_rows * heads_count, key_block.shape[0])
        query_grad = query_grad + jnp.dot(terms, key_block, preferred_element_type=jnp.float32)
        key_grad = lax.dot_general(
            terms, flat_query, (((0,), (0,)), ((), ())), preferred_element_type=jnp.float32
        )
        return (query_grad, key_grad)

    start_grad = jnp.zeros((own_rows * heads_count, width), jnp.float32)
    query_grad, key_grads = lax.scan(back_step, start_grad, (key_blocks, slope_blocks))
    query_grad = query_grad.reshape(own_rows, heads_count, width)
    key_grad = key_grads.reshape(key_count, width)
    out_query = lax.psum_scatter(query_grad, "context", scatter_dimension=1, tiled=True)
    out_key = lax.psum_scatter(key_grad, "heads", scatter_dimension=0, tiled=True)
    return (out_query, out_key)


def solution(mesh):
    placed = (
        P("context", "heads", None),
        P("context", None),
        P(None, "heads"),
        P(),
        P("heads", None, None),
        P("context", None),
        P("heads", None),
    )
    return jax.shard_map(
        on_device,
        mesh=mesh,
        in_specs=placed,
        out_specs=(P("heads", "context", None), P(("context", "heads"), None)),
        check_vma=False,
    )
```

profile of v0, /device:TPU:2, one launch (start us, length us, event | category | flops | bytes accessed | tf_op | source)
XLA Modules:
  0.0 374.9 jit_solution(15053279912884742428)
XLA Ops:
  7.2 0.7 all-gather.2.cloned.1.call-update
  8.0 0.8 reshape.139
  8.8 0.8 dynamic_slice.31
  9.5 0.8 copy.25
  10.3 0.8 mul.63
  11.1 41.8 %all-gather.2.cloned.1.call-done = bf16[256,8,576]{2,1,0:T(8,128)(2,1)} async-done(((bf16[16,8,576]{2,1,0:T(8,128)(2,1)}), bf16[256,8,576]{2,1,0:T(8,128)(2,1)}) %all-gather.2.cloned.1.call-update) | async-done | bytes 2359312 | tf_op jit(solution)/shard_map/all_gather | solution.py:44
  52.9 22.9 %while.36 = (s32[]{:T(128)}, f32[4,64,2048]{2,1,0:T(8,128)}, s32[4,64]{1,0:T(4,128)S(1)}, bf16[4,64,8,576]{3,2,1,0:T(8,128)(2,1)}, bf16[2048,576]{0,1:T(8,128)(2...) while((s32[]{:T(128)}, f32[4,64,2048]{2,1,0:T(8,128)}, s32[4,64]{1,0:T(4,128)S(1)}, ...), condition=%wide.region_8.9_spmd.clone, body=%wide.region_6.8_spmd.clone.sunk | while | flops 1211238400 | bytes 4611937 | solution.py:27
  52.9 4.8 %exponential_reduce_fusion.2 = f32[64,2048]{1,0:T(8,128)S(1)} fusion(bf16[2048,576]{0,1:T(8,128)(2,1)} %get-tuple-element.382, f32[64,8]{1,0:T(8,128)S(1)} %dynamic-slice_bitcast_fusion.5, bf16[4,64,8,576]{3,2,1,0:T(8,128)(2,1)} %get-tuple-element.381, s32[]{:T(128)} %get-tuple-element.370), kind=kOutput, calls=%fused_computation.7.clone.1 | convolution fusion | flops 1210974208 | bytes 3541504 | tf_op jit(solution)/shard_map/while/body/eval_jaxpr/rhd,sd->rhs/dot_general | solution.py:21
  57.7 0.9 fusion.60
  58.6 4.8 %exponential_reduce_fusion.2 = f32[64,2048]{1,0:T(8,128)S(1)} fusion(bf16[2048,576]{0,1:T(8,128)(2,1)} %get-tuple-element.382, f32[64,8]{1,0:T(8,128)S(1)} %dynamic-slice_bitcast_fusion.5, bf16[4,64,8,576]{3,2,1,0:T(8,128)(2,1)} %get-tuple-element.381, s32[]{:T(128)} %get-tuple-element.370), kind=kOutput, calls=%fused_computation.7.clone.1 | convolution fusion | flops 1210974208 | bytes 3541504 | tf_op jit(solution)/shard_map/while/body/eval_jaxpr/rhd,sd->rhs/dot_general | solution.py:21
  63.4 0.9 fusion.60
  64.3 4.8 %exponential_reduce_fusion.2 = f32[64,2048]{1,0:T(8,128)S(1)} fusion(bf16[2048,576]{0,1:T(8,128)(2,1)} %get-tuple-element.382, f32[64,8]{1,0:T(8,128)S(1)} %dynamic-slice_bitcast_fusion.5, bf16[4,64,8,576]{3,2,1,0:T(8,128)(2,1)} %get-tuple-element.381, s32[]{:T(128)} %get-tuple-element.370), kind=kOutput, calls=%fused_computation.7.clone.1 | convolution fusion | flops 1210974208 | bytes 3541504 | tf_op jit(solution)/shard_map/while/body/eval_jaxpr/rhd,sd->rhs/dot_general | solution.py:21
  69.1 0.9 fusion.60
  70.0 4.8 %exponential_reduce_fusion.2 = f32[64,2048]{1,0:T(8,128)S(1)} fusion(bf16[2048,576]{0,1:T(8,128)(2,1)} %get-tuple-element.382, f32[64,8]{1,0:T(8,128)S(1)} %dynamic-slice_bitcast_fusion.5, bf16[4,64,8,576]{3,2,1,0:T(8,128)(2,1)} %get-tuple-element.381, s32[]{:T(128)} %get-tuple-element.370), kind=kOutput, calls=%fused_computation.7.clone.1 | convolution fusion | flops 1210974208 | bytes 3541504 | tf_op jit(solution)/shard_map/while/body/eval_jaxpr/rhd,sd->rhs/dot_general | solution.py:21
  74.8 0.9 fusion.60
  75.8 0.9 copy-done
  76.9 19.8 %while.35 = (s32[]{:T(128)}, f32[4,16,512]{2,1,0:T(8,128)S(1)}, bf16[4,512,128]{2,1,0:T(8,128)(2,1)S(1)}, bf16[1024,128]{1,0:T(8,128)(2,1)S(1)}, f32[16,64]{1,0:T(8,128)S(1)}, /*index=5*/s32[]{:T(128)}) while((s32[]{:T(128)}, f32[4,16,512]{2,1,0:T(8,128)S(1)}, bf16[4,512,128]{2,1,0:T(8,128)(2,1)S(1)}, bf16[1024,128]{1,0:T(8,128)(2,1)S(1)}, ...), condition=%wide.region_1.2_spmd, body=%wide.region_0.1_spmd.sunk | while | flops 141041664 | bytes 8884301 | solution.py:79
  76.9 1.8 maximum_bitcast_fusion.2
  78.7 1.9 copy.41
  80.6 1.2 fusion.56
  81.8 1.8 maximum_bitcast_fusion.2
  83.6 1.9 copy.41
  85.6 1.2 fusion.56
  86.8 1.8 maximum_bitcast_fusion.2
  88.6 1.9 copy.41
  90.5 1.2 fusion.56
  91.8 1.8 maximum_bitcast_fusion.2
  93.6 1.9 copy.41
  95.5 1.2 fusion.56
  97.0 24.9 %pmax.7 = f32[16]{0:T(128)S(1)} all-reduce(f32[16]{0:T(128)S(1)} %fusion.18), channel_id=1, replica_groups=mesh['context'=16,'heads'=16] {'context'}, use_global_device_ids=true, to_apply=%region_3.4 | all-reduce | flops 16 | bytes 128 | tf_op jit(solution)/shard_map/pmax | solution.py:82
  122.1 53.3 %all-reduce.3.cloned.1.call-done = f32[256,2048]{1,0:T(8,128)} async-done(((f32[256,2048]{1,0:T(8,128)}), f32[256,2048]{1,0:T(8,128)}) %all-reduce.3.cloned.1.call-update) | async-done | bytes 2097168 | tf_op jit(solution)/shard_map/psum | solution.py:50
  175.4 1.0 dynamic-slice_reduce_fusion
  176.4 24.2 %all-reduce = (f32[16]{0:T(128)S(1)}, f32[16]{0:T(128)S(1)}) all-reduce(f32[16]{0:T(128)S(1)} %dynamic-slice_reduce_fusion, f32[16]{0:T(128)S(1)} %fusion.19), channel_id=1, replica_groups=mesh['context'=16,'heads'=16] {'context'}, use_global_device_ids=true, to_apply=%region_11.12 | all-reduce | flops 32 | bytes 256 | tf_op jit(solution)/shard_map/psum | solution.py:84
  200.6 1.0 subtract_multiply_fusion
  201.6 0.7 copy.35
  202.3 26.9 %while.37 = (s32[]{:T(128)}, f32[1024,128]{1,0:T(8,128)S(1)}, f32[4,512,128]{2,1,0:T(8,128)}, bf16[4,512,128]{2,1,0:T(8,128)(2,1)S(1)}, bf16[1024,128]{1,0:T(8,1...) while((s32[]{:T(128)}, f32[1024,128]{1,0:T(8,128)S(1)}, ...), condition=%wide.wide.region_13.14_spmd.clone, body=%wide.wide.region_12.13_spmd.clone.sunk | while | flops 405536768 | bytes 13734523 | solution.py:104
  202.3 0.8 dynamic-slice_bitcast_fusion.6
  203.1 0.2 mul.80
  203.3 1.8 copy.42
  205.2 2.1 select_convert_fusion.3
  207.3 0.6 convolution_add_fusion.3
  207.9 1.1 fusion.67
  209.0 0.8 dynamic-slice_bitcast_fusion.6
  209.8 0.2 mul.80
  210.0 1.8 copy.42
  211.9 2.1 select_convert_fusion.3
  214.0 0.6 convolution_add_fusion.3
  214.6 1.1 fusion.67
  215.8 0.8 dynamic-slice_bitcast_fusion.6
  216.5 0.2 mul.80
  216.8 1.8 copy.42
  218.6 2.1 select_convert_fusion.3
  220.7 0.6 convolution_add_fusion.3
  221.3 1.1 fusion.67
  222.5 0.8 dynamic-slice_bitcast_fusion.6
  223.5 1.8 copy.42
  225.3 2.1 select_convert_fusion.3
  227.4 0.6 convolution_add_fusion.3
  228.1 1.2 fusion.67
  229.2 1.1 copy.27
  230.4 0.5 reduce-scatter.5.cloned.1.call-update
  231.0 56.1 %reduce-scatter.3.cloned.1.call-done = f32[16,4,128]{2,0,1:T(8,128)} async-done(((f32[16,64,128]{2,0,1:T(8,128)}), f32[16,4,128]{2,0,1:T(8,128)}) %reduce-scatter.3.cloned.1.call-update) | async-done | bytes 32784 | tf_op jit(solution)/shard_map/reduce_scatter | solution.py:107
  287.1 1.4 copy.28
  288.5 79.9 %reduce-scatter.5.cloned.1.call-done = f32[128,128]{1,0:T(8,128)} async-done(((f32[2048,128]{1,0:T(8,128)}), f32[128,128]{1,0:T(8,128)}) %reduce-scatter.5.cloned.1.call-update) | async-done | bytes 65552 | tf_op jit(solution)/shard_map/reduce_scatter | solution.py:108
  (37 shorter events, 1.2 us)
Async XLA Ops:
  7.2 45.7 %all-gather.2.cloned.1.call-start = ((), (), s32[]{:S(2)}) async-start(), calls=%async_computation.2 | async-start | bytes 2785280 | tf_op jit(solution)/shard_map/all_gather | solution.py:44
  7.9 167.5 %all-reduce.3.cloned.1.call-start = ((), (), s32[]{:S(2)}) async-start(), calls=%async_computation.3 | async-start | bytes 4194304 | tf_op jit(solution)/shard_map/psum | solution.py:50
  75.8 0.9 copy-start
  75.8 1.1 copy-start.1
  75.8 1.1 copy-start.2
  75.8 211.3 %reduce-scatter.3.cloned.1.call-start = ((), (), s32[]{:S(2)}) async-start(), calls=%async_computation.4 | async-start | bytes 557056 | tf_op jit(solution)/shard_map/reduce_scatter | solution.py:107
  230.4 138.0 %reduce-scatter.5.cloned.1.call-start = ((), (), s32[]{:S(2)}) async-start(), calls=%async_computation.5 | async-start | bytes 1114112 | tf_op jit(solution)/shard_map/reduce_scatter | solution.py:108
Sparse Core Ops, SparseCore 0:
  9.8 43.0 all-gather.1
  75.9 99.3 all-reduce.2
  230.5 56.5 reduce-scatter.2
  291.0 77.3 reduce-scatter.4
where the time goes:
time: 376 us; the launch traced here: 375 us
  waiting for transfers between devices  232 us (62%)
  blocking collectives  49.1 us (13%)
  matrix products  46.5 us (12%)
  local copies, waits for them, and re-layouts  26.4 us (7%)
  between operations  13.8 us (4%)
  other arithmetic  6.2 us (2%)
    reduce_scatter x1, waiting for transfers between devices, on_device(): lax.psum_scatter(key_grad, 'heads', scatter_dimension=0, tiled=True)  79.9 us
    reduce_scatter x1, waiting for transfers between devices, on_device(): lax.psum_scatter(query_grad, 'context', scatter_dimension=1, tiled=True)  56.1 us
    psum x1, waiting for transfers between devices, on_device(): summed_mass = lax.psum(partial_mass, 'heads')  53.3 us
    all_gather x1, waiting for transfers between devices, on_device(): lax.all_gather(main_query, 'context', axis=0, tiled=True)  41.8 us
    pmax x1, blocking collectives, on_device(): top = lax.pmax(local_top, 'context')  24.9 us
    psum x1, blocking collectives, on_device(): lax.psum((jnp.sum(weights_exp, axis=1), mass_local), 'context')  24.2 us
    dot_general x4, matrix products, one_block(): jnp.einsum('rhd,sd->rhs', query_block, latent, preferred_element_type=jnp...  19 us
    dot_general x8, matrix products, block_dots(): lax.dot_general(flat_query, key_block, (((1,), (1,)), ((), ())), preferre...  15.5 us
  transfers between devices with their start and end apart: 4, of which 4 were waited for; matrix products, arithmetic and copies ran while one was open for 7% of the time, Pallas kernels for 0%

commit v1 on v0

--- a/solution.py
+++ b/solution.py
@@ -47,7 +47,11 @@
         latent_keys,
         first_key,
     )
-    summed_mass = lax.psum(partial_mass, "heads")
+    summed_mass = partial_mass
+    for hop in (1, 2, 4, 8):
+        summed_mass = summed_mass + lax.ppermute(
+            summed_mass, "heads", [(dev, dev ^ hop) for dev in range(16)]
+        )
     row_mass = lax.dynamic_slice_in_dim(summed_mass, row_first, own_rows, 0)
     own_len = lax.dynamic_slice_in_dim(lengths, row_first, own_rows, 0)
     visible = (first_key + jnp.arange(key_count, dtype=jnp.int32))[None, :] < own_len[:, None]

time: 376 us -> 462 us (1.23)
  waiting for transfers between devices: 232 us -> 318 us
  starting transfers between devices: 0.16 us -> 7.43 us
  local copies, waits for them, and re-layouts: 26.4 us -> 20.5 us
    ppermute x0 -> x4, waiting for transfers between devices: none -> 137 us  [on_device(): lax.ppermute(summed_mass, 'heads', [(dev, dev ^ hop) for dev in range(16)])]
    psum x1 -> x0, waiting for transfers between devices: 53.3 us -> none  [on_device(): summed_mass = lax.psum(partial_mass, 'heads')]
    ppermute x0 -> x4, starting transfers between devices: none -> 7.31 us  [on_device(): lax.ppermute(summed_mass, 'heads', [(dev, dev ^ hop) for dev in range(16)])]
  transfers between devices with their start and end apart: 4 -> 7, of which waited for: 4 -> 7; matrix products, arithmetic and copies ran while one was open for 7% -> 5% of each run, Pallas kernels for 0% -> 0%
where the time goes in v1:
time: 462 us; the launch traced here: 461 us
  waiting for transfers between devices  318 us (69%)
  blocking collectives  48.1 us (10%)
  matrix products  46.4 us (10%)
  local copies, waits for them, and re-layouts  20.5 us (4%)
  between operations  13.8 us (3%)
  starting transfers between devices  7.43 us (2%)
  other arithmetic  6.96 us (2%)
    ppermute x4, waiting for transfers between devices, on_device(): lax.ppermute(summed_mass, 'heads', [(dev, dev ^ hop) for dev in range(16)])  137 us
    reduce_scatter x1, waiting for transfers between devices, on_device(): lax.psum_scatter(key_grad, 'heads', scatter_dimension=0, tiled=True)  80 us
    reduce_scatter x1, waiting for transfers between devices, on_device(): lax.psum_scatter(query_grad, 'context', scatter_dimension=1, tiled=True)  55.3 us
    all_gather x1, waiting for transfers between devices, on_device(): lax.all_gather(main_query, 'context', axis=0, tiled=True)  43.3 us
    pmax x1, blocking collectives, on_device(): top = lax.pmax(local_top, 'context')  24.5 us
    psum x1, blocking collectives, on_device(): lax.psum((jnp.sum(weights_exp, axis=1), mass_local), 'context')  23.5 us
    dot_general x4, matrix products, one_block(): jnp.einsum('rhd,sd->rhs', query_block, latent, preferred_element_type=jnp...  19 us
    dot_general x8, matrix products, block_dots(): lax.dot_general(flat_query, key_block, (((1,), (1,)), ((), ())), preferre...  15.4 us
  transfers between devices with their start and end apart: 7, of which 7 were waited for; matrix products, arithmetic and copies ran while one was open for 5% of the time, Pallas kernels for 0%

profile of v1, /device:TPU:2, one launch (start us, length us, event | category | flops | bytes accessed | tf_op | source)
XLA Modules:
  0.0 461.2 jit_solution(17442033110339471409)
XLA Ops:
  7.2 0.7 all-gather.2.cloned.1.call-update
  8.0 0.8 copy.26
  8.8 0.8 reshape.139
  9.6 43.3 %all-gather.2.cloned.1.call-done = bf16[256,8,576]{2,1,0:T(8,128)(2,1)} async-done(((bf16[16,8,576]{2,1,0:T(8,128)(2,1)}), bf16[256,8,576]{2,1,0:T(8,128)(2,1)}) %all-gather.2.cloned.1.call-update) | async-done | bytes 2359312 | tf_op jit(solution)/shard_map/all_gather | solution.py:44
  52.9 19.7 %while.36 = (s32[]{:T(128)}, f32[4,64,2048]{2,1,0:T(8,128)S(1)}, s32[4,64]{1,0:T(4,128)S(1)}, bf16[4,64,8,576]{3,2,1,0:T(8,128)(2,1)}, bf16[2048,576]{0,1:T(8,12...) while((s32[]{:T(128)}, f32[4,64,2048]{2,1,0:T(8,128)S(1)}, s32[4,64]{1,0:T(4,128)S(1)}, ...), condition=%wide.region_8.9_spmd.clone, body=%wide.region_6.8_spmd.clone.sunk | while | flops 1211238400 | bytes 4611685 | solution.py:27
  52.9 4.8 %exponential_reduce_fusion.2 = f32[64,2048]{1,0:T(8,128)S(1)} fusion(bf16[2048,576]{0,1:T(8,128)(2,1)} %get-tuple-element.382, f32[64,8]{1,0:T(8,128)S(1)} %dynamic-slice_bitcast_fusion.5, bf16[4,64,8,576]{3,2,1,0:T(8,128)(2,1)} %get-tuple-element.381, s32[]{:T(128)} %get-tuple-element.370), kind=kOutput, calls=%fused_computation.7.clone.1 | convolution fusion | flops 1210974208 | bytes 3541504 | tf_op jit(solution)/shard_map/while/body/eval_jaxpr/rhd,sd->rhs/dot_general | solution.py:21
  57.8 4.8 %exponential_reduce_fusion.2 = f32[64,2048]{1,0:T(8,128)S(1)} fusion(bf16[2048,576]{0,1:T(8,128)(2,1)} %get-tuple-element.382, f32[64,8]{1,0:T(8,128)S(1)} %dynamic-slice_bitcast_fusion.5, bf16[4,64,8,576]{3,2,1,0:T(8,128)(2,1)} %get-tuple-element.381, s32[]{:T(128)} %get-tuple-element.370), kind=kOutput, calls=%fused_computation.7.clone.1 | convolution fusion | flops 1210974208 | bytes 3541504 | tf_op jit(solution)/shard_map/while/body/eval_jaxpr/rhd,sd->rhs/dot_general | solution.py:21
  62.8 4.8 %exponential_reduce_fusion.2 = f32[64,2048]{1,0:T(8,128)S(1)} fusion(bf16[2048,576]{0,1:T(8,128)(2,1)} %get-tuple-element.382, f32[64,8]{1,0:T(8,128)S(1)} %dynamic-slice_bitcast_fusion.5, bf16[4,64,8,576]{3,2,1,0:T(8,128)(2,1)} %get-tuple-element.381, s32[]{:T(128)} %get-tuple-element.370), kind=kOutput, calls=%fused_computation.7.clone.1 | convolution fusion | flops 1210974208 | bytes 3541504 | tf_op jit(solution)/shard_map/while/body/eval_jaxpr/rhd,sd->rhs/dot_general | solution.py:21
  67.7 4.8 %exponential_reduce_fusion.2 = f32[64,2048]{1,0:T(8,128)S(1)} fusion(bf16[2048,576]{0,1:T(8,128)(2,1)} %get-tuple-element.382, f32[64,8]{1,0:T(8,128)S(1)} %dynamic-slice_bitcast_fusion.5, bf16[4,64,8,576]{3,2,1,0:T(8,128)(2,1)} %get-tuple-element.381, s32[]{:T(128)} %get-tuple-element.370), kind=kOutput, calls=%fused_computation.7.clone.1 | convolution fusion | flops 1210974208 | bytes 3541504 | tf_op jit(solution)/shard_map/while/body/eval_jaxpr/rhd,sd->rhs/dot_general | solution.py:21
  72.6 1.6 collective-permute-start
  74.2 46.3 %collective-permute-done = f32[256,2048]{1,0:T(8,128)S(1)} collective-permute-done((f32[256,2048]{1,0:T(8,128)S(1)}, f32[256,2048]{1,0:T(8,128)S(1)}, u32[]{:S(2)}, u32[]{:S(2)}) %collective-permute-start) | collective-permute-done | bytes 2097184 | tf_op jit(solution)/shard_map/ppermute | solution.py:52
  120.5 0.3 bitcast_add_fusion
  120.8 3.1 collective-permute-start.1
  123.9 45.4 %collective-permute-done.1 = f32[256,2048]{1,0:T(8,128)S(1)} collective-permute-done((f32[256,2048]{1,0:T(8,128)S(1)}, f32[256,2048]{1,0:T(8,128)S(1)}, u32[]{:S(2)}, u32[]{:S(2)}) %collective-permute-start.1) | collective-permute-done | bytes 2097184 | tf_op jit(solution)/shard_map/ppermute | solution.py:52
  169.3 0.2 add.60
  169.6 0.6 collective-permute-start.2
  170.4 45.5 %collective-permute-done.2 = f32[256,2048]{1,0:T(8,128)} collective-permute-done((f32[256,2048]{1,0:T(8,128)S(1)}, f32[256,2048]{1,0:T(8,128)}, u32[]{:S(2)}, u32[]{:S(2)}) %collective-permute-start.2) | collective-permute-done | bytes 2097184 | tf_op jit(solution)/shard_map/ppermute | solution.py:52
  215.8 3.3 add.61
  219.1 2.0 collective-permute-start.3
  221.1 19.7 %while.35 = (s32[]{:T(128)}, f32[4,16,512]{2,1,0:T(8,128)S(1)}, bf16[4,512,128]{2,1,0:T(8,128)(2,1)S(1)}, bf16[1024,128]{1,0:T(8,128)(2,1)S(1)}, f32[16,64]{1,0:T(8,128)S(1)}, /*index=5*/s32[]{:T(128)}) while((s32[]{:T(128)}, f32[4,16,512]{2,1,0:T(8,128)S(1)}, bf16[4,512,128]{2,1,0:T(8,128)(2,1)S(1)}, bf16[1024,128]{1,0:T(8,128)(2,1)S(1)}, ...), condition=%wide.region_1.2_spmd, body=%wide.region_0.1_spmd.sunk | while | flops 141041664 | bytes 8884301 | solution.py:83
  221.1 1.8 maximum_bitcast_fusion.2
  222.9 1.9 copy.42
  224.8 1.2 fusion.57
  226.1 1.8 maximum_bitcast_fusion.2
  227.8 1.9 copy.42
  229.8 1.2 fusion.57
  231.0 1.8 maximum_bitcast_fusion.2
  232.8 1.9 copy.42
  234.7 1.2 fusion.57
  235.9 1.8 maximum_bitcast_fusion.2
  237.7 1.9 copy.42
  239.6 1.2 fusion.57
  241.1 24.5 %pmax.7 = f32[16]{0:T(128)S(1)} all-reduce(f32[16]{0:T(128)S(1)} %fusion.18), channel_id=1, replica_groups=mesh['context'=16,'heads'=16] {'context'}, use_global_device_ids=true, to_apply=%region_3.4 | all-reduce | flops 16 | bytes 128 | tf_op jit(solution)/shard_map/pmax | solution.py:86
  265.6 0.2 fusion.19
  265.8 0.3 collective-permute-done.3
  266.1 1.1 fusion.21
  267.2 23.5 %all-reduce = (f32[16]{0:T(128)S(1)}, f32[16]{0:T(128)S(1)}) all-reduce(f32[16]{0:T(128)S(1)} %fusion.21, f32[16]{0:T(128)S(1)} %fusion.19), channel_id=1, replica_groups=mesh['context'=16,'heads'=16] {'context'}, use_global_device_ids=true, to_apply=%region_10.11 | all-reduce | flops 32 | bytes 256 | tf_op jit(solution)/shard_map/psum | solution.py:88
  290.8 1.1 subtract_multiply_fusion
  291.9 24.2 %while.37 = (s32[]{:T(128)}, f32[1024,128]{1,0:T(8,128)S(1)}, f32[4,512,128]{2,1,0:T(8,128)}, bf16[4,512,128]{2,1,0:T(8,128)(2,1)S(1)}, bf16[1024,128]{1,0:T(8,1...) while((s32[]{:T(128)}, f32[1024,128]{1,0:T(8,128)S(1)}, ...), condition=%wide.wide.region_12.13_spmd.clone, body=%wide.wide.region_11.12_spmd.clone.sunk | while | flops 405536768 | bytes 13734523 | solution.py:108
  291.9 0.3 mul.80
  292.2 1.9 copy.43
  294.0 2.1 select_convert_fusion.3
  296.1 0.6 convolution_add_fusion.3
  296.8 1.2 fusion.68
  297.9 0.3 mul.80
  298.2 1.9 copy.43
  300.1 2.1 select_convert_fusion.3
  302.2 0.6 convolution_add_fusion.3
  302.8 1.1 fusion.68
  304.0 0.3 mul.80
  304.2 1.9 copy.43
  306.1 2.1 select_convert_fusion.3
  308.2 0.6 convolution_add_fusion.3
  308.9 1.2 fusion.68
  310.0 0.3 mul.80
  310.3 1.9 copy.43
  312.2 2.1 select_convert_fusion.3
  314.3 0.6 convolution_add_fusion.3
  314.9 1.2 fusion.68
  316.1 1.1 copy.28
  317.2 0.7 reduce-scatter.5.cloned.1.call-update
  317.9 55.3 %reduce-scatter.3.cloned.1.call-done = f32[16,4,128]{2,0,1:T(8,128)} async-done(((f32[16,64,128]{2,0,1:T(8,128)}), f32[16,4,128]{2,0,1:T(8,128)}) %reduce-scatter.3.cloned.1.call-update) | async-done | bytes 32784 | tf_op jit(solution)/shard_map/reduce_scatter | solution.py:111
  373.3 1.4 copy.29
  374.6 80.0 %reduce-scatter.5.cloned.1.call-done = f32[128,128]{1,0:T(8,128)} async-done(((f32[2048,128]{1,0:T(8,128)}), f32[128,128]{1,0:T(8,128)}) %reduce-scatter.5.cloned.1.call-update) | async-done | bytes 65552 | tf_op jit(solution)/shard_map/reduce_scatter | solution.py:112
  (47 shorter events, 1.1 us)
Async XLA Ops:
  7.2 45.7 %all-gather.2.cloned.1.call-start = ((), (), s32[]{:S(2)}) async-start(), calls=%async_computation.2 | async-start | bytes 2785280 | tf_op jit(solution)/shard_map/all_gather | solution.py:44
  7.9 365.4 %reduce-scatter.3.cloned.1.call-start = ((), (), s32[]{:S(2)}) async-start(), calls=%async_computation.3 | async-start | bytes 557056 | tf_op jit(solution)/shard_map/reduce_scatter | solution.py:111
  72.6 47.9 %collective-permute-start = (f32[256,2048]{1,0:T(8,128)S(1)}, f32[256,2048]{1,0:T(8,128)S(1)}, u32[]{:S(2)}, u32[]{:S(2)}) collective-permute-start(f32[256,2048]{1,0:T(8,128)S(1)} %bitcast.137), channel_id=1, source_target_pairs={{0,1},{1,0},{2,3},{3,2},{4,5},{5,4},{6,7},{7,6},{8,9},{9,8},{10,11... | collective-permute-start | bytes 6291464 | tf_op jit(solution)/shard_map/ppermute | solution.py:52
  120.8 49.4 %copy-start.3 = (s32[256]{0:T(256)S(1)}, s32[256]{0:T(256)}, u32[]{:S(2)}) copy-start(s32[256]{0:T(256)} %param.16) | copy-start | bytes 3076
  120.8 49.5 %copy-start.2 = (f32[16,64]{1,0:T(8,128)S(1)}, f32[16,64]{1,0:T(8,128)}, u32[]{:S(2)}) copy-start(f32[16,64]{1,0:T(8,128)} %param.19) | copy-start | bytes 12292
  120.8 48.5 %collective-permute-start.1 = (f32[256,2048]{1,0:T(8,128)S(1)}, f32[256,2048]{1,0:T(8,128)S(1)}, u32[]{:S(2)}, u32[]{:S(2)}) collective-permute-start(f32[256,2048]{1,0:T(8,128)S(1)} %bitcast_add_fusion), channel_id=1, source_target_pairs={{0,2},{1,3},{2,0},{3,1},{4,6},{5,7},{6,4},{7,5},{8,10},{9,11},{10,... | collective-permute-start | bytes 6291464 | tf_op jit(solution)/shard_map/ppermute | solution.py:52
  169.6 46.2 %collective-permute-start.2 = (f32[256,2048]{1,0:T(8,128)S(1)}, f32[256,2048]{1,0:T(8,128)}, u32[]{:S(2)}, u32[]{:S(2)}) collective-permute-start(f32[256,2048]{1,0:T(8,128)S(1)} %add.60), channel_id=1, source_target_pairs={{0,4},{1,5},{2,6},{3,7},{4,0},{5,1},{6,2},{7,3},{8,12},{9,13},{10,... | collective-permute-start | bytes 6291464 | tf_op jit(solution)/shard_map/ppermute | solution.py:52
  170.4 50.8 %copy-start = (bf16[16,64,128]{2,1,0:T(8,128)(2,1)S(1)}, bf16[16,64,128]{2,1,0:T(8,128)(2,1)}, u32[]{:S(2)}) copy-start(bf16[16,64,128]{2,1,0:T(8,128)(2,1)} %param.17) | copy-start | bytes 786436
  170.4 50.8 %copy-start.1 = (bf16[2048,128]{1,0:T(8,128)(2,1)S(1)}, bf16[2048,128]{1,0:T(8,128)(2,1)}, u32[]{:S(2)}) copy-start(bf16[2048,128]{1,0:T(8,128)(2,1)} %param.18) | copy-start | bytes 1572868
  219.1 47.0 %collective-permute-start.3 = (f32[256,2048]{1,0:T(8,128)}, f32[256,2048]{1,0:T(8,128)}, u32[]{:S(2)}, u32[]{:S(2)}) collective-permute-start(f32[256,2048]{1,0:T(8,128)} %add.61), channel_id=1, source_target_pairs={{0,8},{1,9},{2,10},{3,11},{4,12},{5,13},{6,14},{7,15},{8,0},{9,1},... | collective-permute-start | bytes 6291464 | tf_op jit(solution)/shard_map/ppermute | solution.py:52
  317.2 137.5 %reduce-scatter.5.cloned.1.call-start = ((), (), s32[]{:S(2)}) async-start(), calls=%async_computation.4 | async-start | bytes 1114112 | tf_op jit(solution)/shard_map/reduce_scatter | solution.py:112
Sparse Core Ops, SparseCore 0:
  9.8 43.0 all-gather.1
  317.3 55.9 reduce-scatter.2
  377.3 77.2 reduce-scatter.4
